TPU v7x, 32 devices: a whole 2x2x4 slice. The times are simulated.
32 devices in a mesh: gx: 2 (over x), gy: 4 (over y, core), gz: 4 (over z).
Axes of the slice: x: 2, y: 2, z: 4, core: 2. Of those that a mesh axis runs over, the one named last changes fastest.
Arguments:
- solution_in: float32 [16, 128, 512], P('gx', 'gy', 'gz'), may hold values from -6 to 6
- residual_in: float32 [16, 128, 512], P('gx', 'gy', 'gz'), may hold values from -12 to 12
- direction_in: float32 [16, 128, 512], P('gx', 'gy', 'gz'), may hold values from -6 to 6
- material: int32 [16, 128, 512], P('gx', 'gy', 'gz'), may hold values from 0 to 7
- cond_table: float32 [8], replicated, may hold values from 0.5 to 4
- cap_table: float32 [8], replicated, may hold values from 0.2 to 1
- gas_flux: float32 [128, 512], P('gy', 'gz'), may hold values from -6 to 6
- supply_map: int32 [128, 512], P('gy', 'gz'), may hold values from 0 to 511, as said below
Outputs:
- solution: float32 [16, 128, 512], P('gx', 'gy', 'gz')
- residual: float32 [16, 128, 512], P('gx', 'gy', 'gz')
- direction: float32 [16, 128, 512], P('gx', 'gy', 'gz')
Inputs may be any that keep to these rules, and one draw needn't show every extreme that they name: `supply_map`: the gas faces are laid out so that the faces held by index q of gz, in their slots t * 128 / 4 to (t + 1) * 128 / 4 - 1, supply solid faces held by index t of gz in the same row; every gas face supplies exactly one solid face of its row.
All inputs are finite; a program needn't handle non-finite values.
Results may differ from a plain program's by a relative error of at most 0.0006.
Values sent between devices are 32-bit elements; how exact they have to be, the bound alone decides.
A program may use at most 64 MiB of HBM per device.

v0:
```python
import jax
import jax.numpy as jnp
from jax import lax
from jax.sharding import PartitionSpec as P

STEPS = 4


def extended(block, sides, width):
    for axis, dim in sides:
        count = lax.axis_size(axis)
        forward = [(i, i + 1) for i in range(count - 1)]
        backward = [(target, source) for source, target in forward]
        low = lax.ppermute(
            lax.slice_in_dim(block, block.shape[dim] - width, None, axis=dim), axis, forward
        )
        high = lax.ppermute(lax.slice_in_dim(block, 0, width, axis=dim), axis, backward)
        block = jnp.concatenate([low, block, high], axis=dim)
    return block


def harmonic(lower_side, upper_side):
    return (
        2.0
        * lower_side
        * upper_side
        / (jnp.where(lower_side > 0, lower_side, 1.0) + jnp.where(upper_side > 0, upper_side, 1.0))
    )


def face_terms(cond):
    return (
        harmonic(cond[:-1], cond[1:]),
        harmonic(cond[:, :-1], cond[:, 1:]),
        harmonic(cond[:, :, :-1], cond[:, :, 1:]),
    )


def operate(values, capacity, conductance):
    result = capacity * values
    face_flow = conductance[0] * (values[1:] - values[:-1])
    result = (
        result
        - jnp.pad(face_flow, ((0, 1), (0, 0), (0, 0)))
        + jnp.pad(face_flow, ((1, 0), (0, 0), (0, 0)))
    )
    face_flow = conductance[1] * (values[:, 1:] - values[:, :-1])
    result = (
        result
        - jnp.pad(face_flow, ((0, 0), (0, 1), (0, 0)))
        + jnp.pad(face_flow, ((0, 0), (1, 0), (0, 0)))
    )
    face_flow = conductance[2] * (values[:, :, 1:] - values[:, :, :-1])
    result = (
        result
        - jnp.pad(face_flow, ((0, 0), (0, 0), (0, 1)))
        + jnp.pad(face_flow, ((0, 0), (0, 0), (1, 0)))
    )
    return result


def lookup_code(codes, table):
    summed = jnp.zeros(codes.shape, jnp.float32)
    for material_id in range(table.shape[0]):
        summed = summed + jnp.where(
            codes == jnp.float32(material_id + 1), table[material_id], jnp.float32(0.0)
        )
    return summed


def spectrum(cond_table, cap_table):
    lowest = jnp.min(cap_table)
    highest = jnp.max(cap_table) + 12.0 * jnp.max(cond_table)
    return (0.5 * (highest + lowest), 0.5 * (highest - lowest))


def next_term(applied, terms, center, half_width):
    shifted = (applied - center * terms[-1]) / half_width
    if len(terms) == 1:
        return shifted
    return 2.0 * shifted - terms[-2]


def shift_matrix(center, half_width, steps):
    dimension = 2 * steps + 1
    matrix = jnp.zeros((dimension, dimension), jnp.float32)
    for offset, length in ((0, steps + 1), (steps + 1, steps)):
        for column in range(length - 1):
            matrix = matrix.at[offset + column, offset + column].set(center)
            matrix = matrix.at[offset + column + 1, offset + column].set(
                half_width if column == 0 else 0.5 * half_width
            )
            if column >= 1:
                matrix = matrix.at[offset + column - 1, offset + column].set(0.5 * half_width)
    return matrix


def coefficients(gram, center, half_width, steps):
    dimension = 2 * steps + 1
    matrix = shift_matrix(center, half_width, steps)
    highest_prec = lax.Precision.HIGHEST

    def gram_product(first_vec, second_vec):
        return jnp.dot(
            first_vec, jnp.dot(gram, second_vec, precision=highest_prec), precision=highest_prec
        )

    direct = jnp.zeros((dimension,), jnp.float32).at[0].set(1.0)
    residue = jnp.zeros((dimension,), jnp.float32).at[steps + 1].set(1.0)
    moved = jnp.zeros((dimension,), jnp.float32)
    norm_now = gram_product(residue, residue)
    for sweep in range(steps):
        mapped = jnp.dot(matrix, direct, precision=highest_prec)
        step_length = norm_now / gram_product(direct, mapped)
        moved = moved + step_length * direct
        residue = residue - step_length * mapped
        norm_next = gram_product(residue, residue)
        direct = residue + norm_next / norm_now * direct
        norm_now = norm_next
    return (moved, residue, direct)


def combine(weights, basis):
    summed = weights[0] * basis[0]
    for position in range(1, len(basis)):
        summed = summed + weights[position] * basis[position]
    return summed


def inside(values, depth):
    return values[depth:-depth, depth:-depth, depth:-depth]


def body(
    solution_in, residual_in, direction_in, material, cond_table, cap_table, gas_flux, supply_map
):
    surface_rows, surface_width = gas_flux.shape
    groups = lax.axis_size("gz")
    segment = surface_width // groups
    arrived = lax.all_to_all(
        gas_flux.reshape(surface_rows, groups, segment),
        "gz",
        split_axis=1,
        concat_axis=1,
        tiled=True,
    )
    arrived = arrived.reshape(surface_rows, surface_width)
    slot = (
        supply_map // surface_width * segment
        + supply_map % surface_width
        - lax.axis_index("gz") * segment
    )
    incoming = jnp.take_along_axis(arrived, slot, axis=1)
    is_top = lax.axis_index("gx") == lax.axis_size("gx") - 1
    start = residual_in.at[-1].add(jnp.where(is_top, incoming, jnp.float32(0.0)))
    codes = (material + 1).astype(jnp.float32)
    center, half_width = spectrum(cond_table, cap_table)
    first = extended(jnp.stack([direction_in, start, codes]), (("gx", 1), ("gy", 2), ("gz", 3)), 1)
    conductance = face_terms(lookup_code(first[2], cond_table))
    capacity_ext = lookup_code(first[2], cap_table)
    dir_terms = [direction_in]
    res_terms = [start]
    dir_applied = inside(operate(first[0], capacity_ext, conductance), 1)
    res_applied = inside(operate(first[1], capacity_ext, conductance), 1)
    res_terms.append(next_term(res_applied, res_terms, center, half_width))
    dir_terms.append(next_term(dir_applied, dir_terms, center, half_width))
    for sweep in range(1, STEPS):
        if sweep < STEPS - 1:
            layered = extended(
                jnp.stack([dir_terms[-1], res_terms[-1]]), (("gx", 1), ("gy", 2), ("gz", 3)), 1
            )
            dir_applied = inside(operate(layered[0], capacity_ext, conductance), 1)
            res_applied = inside(operate(layered[1], capacity_ext, conductance), 1)
            res_terms.append(next_term(res_applied, res_terms, center, half_width))
        else:
            layered = extended(dir_terms[-1], (("gx", 0), ("gy", 1), ("gz", 2)), 1)
            dir_applied = inside(operate(layered, capacity_ext, conductance), 1)
        dir_terms.append(next_term(dir_applied, dir_terms, center, half_width))
    basis = dir_terms + res_terms
    stacked = jnp.stack([term.reshape(-1) for term in basis])
    partial_gram = jnp.dot(stacked, stacked.T, precision=lax.Precision.HIGHEST)
    gram = lax.psum(partial_gram, ("gx", "gy", "gz"))
    moved, residue, direct = coefficients(gram, center, half_width, STEPS)
    return (solution_in + combine(moved, basis), combine(residue, basis), combine(direct, basis))


def solution(mesh):
    in_specs = (
        P("gx", "gy", "gz"),
        P("gx", "gy", "gz"),
        P("gx", "gy", "gz"),
        P("gx", "gy", "gz"),
        P(),
        P(),
        P("gy", "gz"),
        P("gy", "gz"),
    )
    out_specs = (P("gx", "gy", "gz"), P("gx", "gy", "gz"), P("gx", "gy", "gz"))
    return jax.shard_map(body, mesh=mesh, in_specs=in_specs, out_specs=out_specs, check_vma=False)
```

profile of v0, /device:TPU:0, one launch (start us, length us, event | category | flops | bytes accessed | tf_op | source)
XLA Modules:
  0.0 260.0 jit_solution(15775123754584945129)
XLA Ops:
  2.2 6.3 %all-to-all-start = ((f32[4,1,1024]{2,1,0:T(1,128)}), f32[4,1,1024]{2,1,0:T(1,128)S(1)}, u32[]{:S(2)}, u32[]{:S(2)}) async-start(f32[4,1,1024]{2,1,0:T(1,128)} %reshape.745), calls=%async_computation | async-start | bytes 32768 | tf_op jit(solution)/shard_map/all_to_all | solution.py:140
  10.2 3.9 %all-to-all-done = f32[4,1,1024]{2,1,0:T(1,128)S(1)} async-done(((f32[4,1,1024]{2,1,0:T(1,128)}), f32[4,1,1024]{2,1,0:T(1,128)S(1)}, u32[]{:S(2)}, u32[]{:S(2)}) %all-to-all-start) | async-done | bytes 16416 | tf_op jit(solution)/shard_map/all_to_all | solution.py:140
  15.6 25.6 %gather_fusion = f32[4096]{0:T(1024)S(1)} fusion(f32[32,128]{1,0:T(8,128)S(1)} %reshape.660, s32[4096]{0:T(1024)S(1)} %fusion.80), kind=kCustom, calls=%fused_computation | custom fusion | bytes 65536 | tf_op jit(solution)/shard_map/jit(take_along_axis)/gather | solution.py:153
  41.3 3.4 %collective-permute-start = (f32[3,1,32,128]{3,2,1,0:T(8,128)S(1)}, f32[3,1,32,128]{3,2,1,0:T(8,128)S(1)}, u32[]{:S(2)}, u32[]{:S(2)}) collective-permute-start(f32[3,1,32,128]{3,2,1,0:T(8,128)S(1)} %get-tuple-element.320), channel_id=1, source_target_pairs={{0,16},{1,17},{2,18},{3,19},{4,20},{5,21},{6,22},{7,23},{8,24},{9,... | collective-permute-start | bytes 147464 | tf_op jit(solution)/shard_map/ppermute | solution.py:14
  46.7 4.0 %collective-permute-done.1 = f32[3,1,32,128]{3,2,1,0:T(8,128)S(1)} collective-permute-done((f32[3,1,32,128]{3,2,1,0:T(8,128)S(1)}, f32[3,1,32,128]{3,2,1,0:T(8,128)S(1)}, u32[]{:S(2)}, u32[]{:S(2)}) %collective-permute-start.1) | collective-permute-done | bytes 49184 | tf_op jit(solution)/shard_map/ppermute | solution.py:17
  54.0 2.8 %collective-permute-done.3 = f32[3,10,1,128]{3,2,1,0:T(1,128)S(1)} collective-permute-done((f32[3,10,1,128]{3,2,1,0:T(1,128)S(1)}, f32[3,10,1,128]{3,2,1,0:T(1,128)S(1)}, u32[]{:S(2)}, u32[]{:S(2)}) %collective-permute-start.3) | collective-permute-done | bytes 15392 | tf_op jit(solution)/shard_map/ppermute | solution.py:17
  57.4 2.6 collective-permute-start.4
  67.0 5.8 %bitcast_multiply_fusion.6 = (f32[10,34,130]{2,1,0:T(8,128)S(1)}, f32[1,10,34,130]{3,2,1,0:T(8,128)S(1)}, pred[1,10,34,130]{3,2,1,0:T(8,128)(4,1)S(1)}, pred[1,1...) fusion(f32[3,10,34,130]{3,2,1,0:T(8,128)S(1)} %pad_maximum_fusi, ...), kind=kLoop, calls=%fused_computation.85 | loop fusion | flops 1060800 | bytes 1060832 | tf_op jit(solution)/shard_map/mul | solution.py:40
  72.8 5.4 %add_add_fusion = f32[1,10,34,130]{3,2,1,0:T(8,128)S(1)} fusion(pred[1,10,34,130]{3,2,1,0:T(8,128)(4,1)S(1)} %get-tuple-element.283, pred[1,10,34,130]{3,2,1,0:T(8,128)(4,1)S(1)} %get-tuple-element.282, pred[1,10,34,130]{3,2,1,0:T(8,128)(4,1)S(1)} %get-tuple-element.281, pred[1,10,34,130]{3,2,1,0:T(8,128)(4,1)S(1)} %get-tuple-element.280, ...), kind=kLoop, calls=%fused_computation.86 | loop fusion | flops 663000 | bytes 530432 | tf_op jit(solution)/shard_map/add | solution.py:65
  82.8 4.2 %collective-permute-done.7 = f32[2,1,32,128]{3,2,1,0:T(8,128)S(1)} collective-permute-done((f32[2,1,32,128]{3,2,1,0:T(8,128)S(1)}, f32[2,1,32,128]{3,2,1,0:T(8,128)S(1)}, u32[]{:S(2)}, u32[]{:S(2)}) %collective-permute-start.7) | collective-permute-done | bytes 32800 | tf_op jit(solution)/shard_map/ppermute | solution.py:17
  87.1 2.4 collective-permute-start.8
  90.8 3.3 %collective-permute-done.9 = f32[2,10,1,128]{3,2,1,0:T(1,128)S(1)} collective-permute-done((f32[2,10,1,128]{3,2,1,0:T(1,128)S(1)}, f32[2,10,1,128]{3,2,1,0:T(1,128)S(1)}, u32[]{:S(2)}, u32[]{:S(2)}) %collective-permute-start.9) | collective-permute-done | bytes 10272 | tf_op jit(solution)/shard_map/ppermute | solution.py:17
  94.3 4.3 %collective-permute-start.10 = (f32[2,10,34,1]{3,2,1,0:T(8,128)S(1)}, f32[2,10,34,1]{3,2,1,0:T(8,128)S(1)}, u32[]{:S(2)}, u32[]{:S(2)}) collective-permute-start(f32[2,10,34,1]{3,2,1,0:T(8,128)S(1)} %get-tuple-element.318), channel_id=1, source_target_pairs={{0,1},{1,2},{2,3},{4,5},{5,6},{6,7},{8,9},{9,10},{10,11},{12,13},{... | collective-permute-start | bytes 8168 | tf_op jit(solution)/shard_map/ppermute | solution.py:14
  99.9 7.0 %collective-permute-done.10 = f32[2,10,34,1]{3,2,1,0:T(8,128)S(1)} collective-permute-done((f32[2,10,34,1]{3,2,1,0:T(8,128)S(1)}, f32[2,10,34,1]{3,2,1,0:T(8,128)S(1)}, u32[]{:S(2)}, u32[]{:S(2)}) %collective-permute-start.10) | collective-permute-done | bytes 2752 | tf_op jit(solution)/shard_map/ppermute | solution.py:14
  106.9 4.7 %collective-permute-done.11 = f32[2,10,34,1]{3,2,1,0:T(8,128)S(1)} collective-permute-done((f32[2,10,34,1]{3,2,1,0:T(8,128)S(1)}, f32[2,10,34,1]{3,2,1,0:T(8,128)S(1)}, u32[]{:S(2)}, u32[]{:S(2)}) %collective-permute-start.11) | collective-permute-done | bytes 2752 | tf_op jit(solution)/shard_map/ppermute | solution.py:17
  116.7 4.2 %collective-permute-done.13 = f32[2,1,32,128]{3,2,1,0:T(8,128)S(1)} collective-permute-done((f32[2,1,32,128]{3,2,1,0:T(8,128)S(1)}, f32[2,1,32,128]{3,2,1,0:T(8,128)S(1)}, u32[]{:S(2)}, u32[]{:S(2)}) %collective-permute-start.13) | collective-permute-done | bytes 32800 | tf_op jit(solution)/shard_map/ppermute | solution.py:17
  120.9 1.8 collective-permute-start.14
  124.0 1.9 collective-permute-done.15
  126.2 2.4 collective-permute-start.16
  129.9 7.0 %collective-permute-done.16 = f32[2,10,34,1]{3,2,1,0:T(8,128)S(1)} collective-permute-done((f32[2,10,34,1]{3,2,1,0:T(8,128)S(1)}, f32[2,10,34,1]{3,2,1,0:T(8,128)S(1)}, u32[]{:S(2)}, u32[]{:S(2)}) %collective-permute-start.16) | collective-permute-done | bytes 2752 | tf_op jit(solution)/shard_map/ppermute | solution.py:14
  136.9 4.7 %collective-permute-done.17 = f32[2,10,34,1]{3,2,1,0:T(8,128)S(1)} collective-permute-done((f32[2,10,34,1]{3,2,1,0:T(8,128)S(1)}, f32[2,10,34,1]{3,2,1,0:T(8,128)S(1)}, u32[]{:S(2)}, u32[]{:S(2)}) %collective-permute-start.17) | collective-permute-done | bytes 2752 | tf_op jit(solution)/shard_map/ppermute | solution.py:17
  147.5 4.2 %collective-permute-done.19 = f32[1,32,128]{2,1,0:T(8,128)S(1)} collective-permute-done((f32[1,32,128]{2,1,0:T(8,128)S(1)}, f32[1,32,128]{2,1,0:T(8,128)S(1)}, u32[]{:S(2)}, u32[]{:S(2)}) %collective-permute-start.19) | collective-permute-done | bytes 16416 | tf_op jit(solution)/shard_map/ppermute | solution.py:17
  156.1 1.9 dynamic-slice.147
  163.1 2.5 collective-permute-start.22
  167.0 3.3 %collective-permute-done.22 = f32[10,34,1]{2,1,0:T(8,128)S(1)} collective-permute-done((f32[10,34,1]{2,1,0:T(8,128)S(1)}, f32[10,34,1]{2,1,0:T(8,128)S(1)}, u32[]{:S(2)}, u32[]{:S(2)}) %collective-permute-start.22) | collective-permute-done | bytes 1392 | tf_op jit(solution)/shard_map/ppermute | solution.py:14
  170.3 4.7 %collective-permute-done.23 = f32[10,34,1]{2,1,0:T(8,128)S(1)} collective-permute-done((f32[10,34,1]{2,1,0:T(8,128)S(1)}, f32[10,34,1]{2,1,0:T(8,128)S(1)}, u32[]{:S(2)}, u32[]{:S(2)}) %collective-permute-start.23) | collective-permute-done | bytes 1392 | tf_op jit(solution)/shard_map/ppermute | solution.py:17
  178.1 1.9 stack.43
  180.0 2.9 %fusion.119 = f32[9,9]{1,0:T(8,128)S(1)} fusion(f32[9,32768]{1,0:T(8,128)S(1)} %stack.43), kind=kOutput, calls=%fused_computation.275 | convolution fusion | flops 31850496 | bytes 1179972 | tf_op jit(solution)/shard_map/dot_general | solution.py:181
  183.0 38.1 %psum.7 = f32[9,9]{1,0:T(8,128)S(1)} all-reduce(f32[9,9]{1,0:T(8,128)S(1)} %fusion.119), channel_id=1, replica_groups=mesh['gx'=2,'gy'=4,'gz'=4] {'gx','gy','gz'}, use_global_device_ids=true, to_apply=%region_3.4 | all-reduce | flops 81 | bytes 648 | tf_op jit(solution)/shard_map/psum | solution.py:182
  240.9 6.2 %multiply_add_fusion = f32[8,32,128]{2,1,0:T(8,128)} fusion(f32[8,32,128]{2,1,0:T(8,128)S(1)} %fusion.54, f32[8,32,128]{2,1,0:T(8,128)S(1)} %fusion.66, f32[8,32,128]{2,1,0:T(8,128)S(1)} %get-tuple-element.383, f32[8,32,128]{2,1,0:T(8,128)S(1)} %fusion.78, f32[8,32,128]{2,1,0:T(8,128)S(1)} %fusion.58, f32[8,32,128]{2,1,0:T(8,128)S(1)} %fusion.62, ...), kind=kLoop, calls=%fused_computation.187 | loop fusion | flops 557056 | bytes 1310756 | tf_op jit(solution)/shard_map/add | solution.py:126
  247.2 6.4 %multiply_add_fusion.1 = f32[8,32,128]{2,1,0:T(8,128)} fusion(f32[8,32,128]{2,1,0:T(8,128)S(1)} %fusion.54, f32[8,32,128]{2,1,0:T(8,128)S(1)} %fusion.66, f32[8,32,128]{2,1,0:T(8,128)S(1)} %get-tuple-element.383, f32[8,32,128]{2,1,0:T(8,128)S(1)} %fusion.78, f32[8,32,128]{2,1,0:T(8,128)S(1)} %fusion.58, f32[8,32,128]{2,1,0:T(8,128)S(1)} %fusion.62, ...), kind=kLoop, calls=%fused_computation.188 | loop fusion | flops 557056 | bytes 1310756 | tf_op jit(solution)/shard_map/add | solution.py:126
  253.6 6.4 %add_add_fusion.2 = f32[8,32,128]{2,1,0:T(8,128)} fusion(f32[8,32,128]{2,1,0:T(8,128)S(1)} %copy-done.3, f32[8,32,128]{2,1,0:T(8,128)S(1)} %fusion.54, f32[8,32,128]{2,1,0:T(8,128)S(1)} %fusion.66, f32[8,32,128]{2,1,0:T(8,128)S(1)} %get-tuple-element.383, f32[8,32,128]{2,1,0:T(8,128)S(1)} %fusion.78, f32[8,32,128]{2,1,0:T(8,128)S(1)} %fusion.58, ...), kind=kLoop, calls=%fused_computation.189 | loop fusion | flops 589824 | bytes 1441828 | tf_op jit(solution)/shard_map/add | solution.py:184
  (161 shorter events, 57.8 us)
Async XLA Ops:
  2.2 11.9 %all-to-all-start = ((f32[4,1,1024]{2,1,0:T(1,128)}), f32[4,1,1024]{2,1,0:T(1,128)S(1)}, u32[]{:S(2)}, u32[]{:S(2)}) async-start(f32[4,1,1024]{2,1,0:T(1,128)} %reshape.745), calls=%async_computation | async-start | bytes 32768 | tf_op jit(solution)/shard_map/all_to_all | solution.py:140
  15.5 25.7 %copy-start = (f32[8,32,128]{2,1,0:T(8,128)S(1)}, f32[8,32,128]{2,1,0:T(8,128)}, u32[]{:S(2)}) copy-start(f32[8,32,128]{2,1,0:T(8,128)} %param.53) | copy-start | bytes 393220
  15.6 25.7 %copy-start.1 = (f32[8,32,128]{2,1,0:T(8,128)S(1)}, f32[8,32,128]{2,1,0:T(8,128)}, u32[]{:S(2)}) copy-start(f32[8,32,128]{2,1,0:T(8,128)} %param.54) | copy-start | bytes 393220
  15.6 30.4 %copy-start.5 = (f32[8]{0:T(128)S(1)}, f32[8]{0:T(128)}, u32[]{:S(2)}) copy-start(f32[8]{0:T(128)} %param.57) | copy-start | bytes 100
  15.6 37.7 %copy-start.6 = (f32[8]{0:T(128)S(1)}, f32[8]{0:T(128)}, u32[]{:S(2)}) copy-start(f32[8]{0:T(128)} %param.56) | copy-start | bytes 100
  41.3 5.4 %collective-permute-start = (f32[3,1,32,128]{3,2,1,0:T(8,128)S(1)}, f32[3,1,32,128]{3,2,1,0:T(8,128)S(1)}, u32[]{:S(2)}, u32[]{:S(2)}) collective-permute-start(f32[3,1,32,128]{3,2,1,0:T(8,128)S(1)} %get-tuple-element.320), channel_id=1, source_target_pairs={{0,16},{1,17},{2,18},{3,19},{4,20},{5,21},{6,22},{7,23},{8,24},{9,... | collective-permute-start | bytes 147464 | tf_op jit(solution)/shard_map/ppermute | solution.py:14
  44.7 6.0 %collective-permute-start.1 = (f32[3,1,32,128]{3,2,1,0:T(8,128)S(1)}, f32[3,1,32,128]{3,2,1,0:T(8,128)S(1)}, u32[]{:S(2)}, u32[]{:S(2)}) collective-permute-start(f32[3,1,32,128]{3,2,1,0:T(8,128)S(1)} %get-tuple-element.321), channel_id=1, source_target_pairs={{16,0},{17,1},{18,2},{19,3},{20,4},{21,5},{22,6},{23,7},{24,8},{25... | collective-permute-start | bytes 147464 | tf_op jit(solution)/shard_map/ppermute | solution.py:17
  50.7 3.3 %collective-permute-start.2 = (f32[3,10,1,128]{3,2,1,0:T(1,128)S(1)}, f32[3,10,1,128]{3,2,1,0:T(1,128)S(1)}, u32[]{:S(2)}, u32[]{:S(2)}) collective-permute-start(f32[3,10,1,128]{3,2,1,0:T(1,128)S(1)} %get-tuple-element.306), channel_id=1, source_target_pairs={{0,4},{4,8},{8,12},{1,5},{5,9},{9,13},{2,6},{6,10},{10,14},{3,7},{... | collective-permute-start | bytes 46088 | tf_op jit(solution)/shard_map/ppermute | solution.py:14
  52.0 4.8 %collective-permute-start.3 = (f32[3,10,1,128]{3,2,1,0:T(1,128)S(1)}, f32[3,10,1,128]{3,2,1,0:T(1,128)S(1)}, u32[]{:S(2)}, u32[]{:S(2)}) collective-permute-start(f32[3,10,1,128]{3,2,1,0:T(1,128)S(1)} %get-tuple-element.307), channel_id=1, source_target_pairs={{4,0},{8,4},{12,8},{5,1},{9,5},{13,9},{6,2},{10,6},{14,10},{7,3},{... | collective-permute-start | bytes 46088 | tf_op jit(solution)/shard_map/ppermute | solution.py:17
  57.4 7.8 %collective-permute-start.4 = (f32[3,10,34,1]{2,3,1,0:T(1,128)S(1)}, f32[3,10,34,1]{2,3,1,0:T(1,128)S(1)}, u32[]{:S(2)}, u32[]{:S(2)}) collective-permute-start(f32[3,10,34,1]{2,3,1,0:T(1,128)S(1)} %copy.31), channel_id=1, source_target_pairs={{0,1},{1,2},{2,3},{4,5},{5,6},{6,7},{8,9},{9,10},{10,11},{12,13},{... | collective-permute-start | bytes 12248 | tf_op jit(solution)/shard_map/ppermute | solution.py:14
  60.3 5.6 %collective-permute-start.5 = (f32[3,10,34,1]{2,3,1,0:T(1,128)S(1)}, f32[3,10,34,1]{2,3,1,0:T(1,128)S(1)}, u32[]{:S(2)}, u32[]{:S(2)}) collective-permute-start(f32[3,10,34,1]{2,3,1,0:T(1,128)S(1)} %copy.32), channel_id=1, source_target_pairs={{1,0},{2,1},{3,2},{5,4},{6,5},{7,6},{9,8},{10,9},{11,10},{13,12},{... | collective-permute-start | bytes 12248 | tf_op jit(solution)/shard_map/ppermute | solution.py:17
  79.7 3.2 %collective-permute-start.6 = (f32[2,1,32,128]{3,2,1,0:T(8,128)S(1)}, f32[2,1,32,128]{3,2,1,0:T(8,128)S(1)}, u32[]{:S(2)}, u32[]{:S(2)}) collective-permute-start(f32[2,1,32,128]{3,2,1,0:T(8,128)S(1)} %get-tuple-element.328), channel_id=1, source_target_pairs={{0,16},{1,17},{2,18},{3,19},{4,20},{5,21},{6,22},{7,23},{8,24},{9,... | collective-permute-start | bytes 98312 | tf_op jit(solution)/shard_map/ppermute | solution.py:14
  81.3 5.8 %collective-permute-start.7 = (f32[2,1,32,128]{3,2,1,0:T(8,128)S(1)}, f32[2,1,32,128]{3,2,1,0:T(8,128)S(1)}, u32[]{:S(2)}, u32[]{:S(2)}) collective-permute-start(f32[2,1,32,128]{3,2,1,0:T(8,128)S(1)} %get-tuple-element.329), channel_id=1, source_target_pairs={{16,0},{17,1},{18,2},{19,3},{20,4},{21,5},{22,6},{23,7},{24,8},{25... | collective-permute-start | bytes 98312 | tf_op jit(solution)/shard_map/ppermute | solution.py:17
  87.1 3.7 %collective-permute-start.8 = (f32[2,10,1,128]{3,2,1,0:T(1,128)S(1)}, f32[2,10,1,128]{3,2,1,0:T(1,128)S(1)}, u32[]{:S(2)}, u32[]{:S(2)}) collective-permute-start(f32[2,10,1,128]{3,2,1,0:T(1,128)S(1)} %get-tuple-element.324), channel_id=1, source_target_pairs={{0,4},{4,8},{8,12},{1,5},{5,9},{9,13},{2,6},{6,10},{10,14},{3,7},{... | collective-permute-start | bytes 30728 | tf_op jit(solution)/shard_map/ppermute | solution.py:14
  89.5 4.6 %collective-permute-start.9 = (f32[2,10,1,128]{3,2,1,0:T(1,128)S(1)}, f32[2,10,1,128]{3,2,1,0:T(1,128)S(1)}, u32[]{:S(2)}, u32[]{:S(2)}) collective-permute-start(f32[2,10,1,128]{3,2,1,0:T(1,128)S(1)} %get-tuple-element.325), channel_id=1, source_target_pairs={{4,0},{8,4},{12,8},{5,1},{9,5},{13,9},{6,2},{10,6},{14,10},{7,3},{... | collective-permute-start | bytes 30728 | tf_op jit(solution)/shard_map/ppermute | solution.py:17
  94.3 12.6 %collective-permute-start.10 = (f32[2,10,34,1]{3,2,1,0:T(8,128)S(1)}, f32[2,10,34,1]{3,2,1,0:T(8,128)S(1)}, u32[]{:S(2)}, u32[]{:S(2)}) collective-permute-start(f32[2,10,34,1]{3,2,1,0:T(8,128)S(1)} %get-tuple-element.318), channel_id=1, source_target_pairs={{0,1},{1,2},{2,3},{4,5},{5,6},{6,7},{8,9},{9,10},{10,11},{12,13},{... | collective-permute-start | bytes 8168 | tf_op jit(solution)/shard_map/ppermute | solution.py:14
  98.6 13.0 %collective-permute-start.11 = (f32[2,10,34,1]{3,2,1,0:T(8,128)S(1)}, f32[2,10,34,1]{3,2,1,0:T(8,128)S(1)}, u32[]{:S(2)}, u32[]{:S(2)}) collective-permute-start(f32[2,10,34,1]{3,2,1,0:T(8,128)S(1)} %get-tuple-element.319), channel_id=1, source_target_pairs={{1,0},{2,1},{3,2},{5,4},{6,5},{7,6},{9,8},{10,9},{11,10},{13,12},{... | collective-permute-start | bytes 8168 | tf_op jit(solution)/shard_map/ppermute | solution.py:17
  113.4 3.3 %collective-permute-start.12 = (f32[2,1,32,128]{3,2,1,0:T(8,128)S(1)}, f32[2,1,32,128]{3,2,1,0:T(8,128)S(1)}, u32[]{:S(2)}, u32[]{:S(2)}) collective-permute-start(f32[2,1,32,128]{3,2,1,0:T(8,128)S(1)} %get-tuple-element.326), channel_id=1, source_target_pairs={{0,16},{1,17},{2,18},{3,19},{4,20},{5,21},{6,22},{7,23},{8,24},{9,... | collective-permute-start | bytes 98312 | tf_op jit(solution)/shard_map/ppermute | solution.py:14
  115.0 5.9 %collective-permute-start.13 = (f32[2,1,32,128]{3,2,1,0:T(8,128)S(1)}, f32[2,1,32,128]{3,2,1,0:T(8,128)S(1)}, u32[]{:S(2)}, u32[]{:S(2)}) collective-permute-start(f32[2,1,32,128]{3,2,1,0:T(8,128)S(1)} %get-tuple-element.327), channel_id=1, source_target_pairs={{16,0},{17,1},{18,2},{19,3},{20,4},{21,5},{22,6},{23,7},{24,8},{25... | collective-permute-start | bytes 98312 | tf_op jit(solution)/shard_map/ppermute | solution.py:17
  120.9 3.1 %collective-permute-start.14 = (f32[2,10,1,128]{3,2,1,0:T(1,128)S(1)}, f32[2,10,1,128]{3,2,1,0:T(1,128)S(1)}, u32[]{:S(2)}, u32[]{:S(2)}) collective-permute-start(f32[2,10,1,128]{3,2,1,0:T(1,128)S(1)} %get-tuple-element.322), channel_id=1, source_target_pairs={{0,4},{4,8},{8,12},{1,5},{5,9},{9,13},{2,6},{6,10},{10,14},{3,7},{... | collective-permute-start | bytes 30728 | tf_op jit(solution)/shard_map/ppermute | solution.py:14
  122.7 3.2 %collective-permute-start.15 = (f32[2,10,1,128]{3,2,1,0:T(1,128)S(1)}, f32[2,10,1,128]{3,2,1,0:T(1,128)S(1)}, u32[]{:S(2)}, u32[]{:S(2)}) collective-permute-start(f32[2,10,1,128]{3,2,1,0:T(1,128)S(1)} %get-tuple-element.323), channel_id=1, source_target_pairs={{4,0},{8,4},{12,8},{5,1},{9,5},{13,9},{6,2},{10,6},{14,10},{7,3},{... | collective-permute-start | bytes 30728 | tf_op jit(solution)/shard_map/ppermute | solution.py:17
  126.2 10.7 %collective-permute-start.16 = (f32[2,10,34,1]{3,2,1,0:T(8,128)S(1)}, f32[2,10,34,1]{3,2,1,0:T(8,128)S(1)}, u32[]{:S(2)}, u32[]{:S(2)}) collective-permute-start(f32[2,10,34,1]{3,2,1,0:T(8,128)S(1)} %get-tuple-element.312), channel_id=1, source_target_pairs={{0,1},{1,2},{2,3},{4,5},{5,6},{6,7},{8,9},{9,10},{10,11},{12,13},{... | collective-permute-start | bytes 8168 | tf_op jit(solution)/shard_map/ppermute | solution.py:14
  128.6 13.0 %collective-permute-start.17 = (f32[2,10,34,1]{3,2,1,0:T(8,128)S(1)}, f32[2,10,34,1]{3,2,1,0:T(8,128)S(1)}, u32[]{:S(2)}, u32[]{:S(2)}) collective-permute-start(f32[2,10,34,1]{3,2,1,0:T(8,128)S(1)} %get-tuple-element.313), channel_id=1, source_target_pairs={{1,0},{2,1},{3,2},{5,4},{6,5},{7,6},{9,8},{10,9},{11,10},{13,12},{... | collective-permute-start | bytes 8168 | tf_op jit(solution)/shard_map/ppermute | solution.py:17
  144.4 3.0 %collective-permute-start.18 = (f32[1,32,128]{2,1,0:T(8,128)S(1)}, f32[1,32,128]{2,1,0:T(8,128)S(1)}, u32[]{:S(2)}, u32[]{:S(2)}) collective-permute-start(f32[1,32,128]{2,1,0:T(8,128)S(1)} %get-tuple-element.334), channel_id=1, source_target_pairs={{0,16},{1,17},{2,18},{3,19},{4,20},{5,21},{6,22},{7,23},{8,24},{9,... | collective-permute-start | bytes 49160 | tf_op jit(solution)/shard_map/ppermute | solution.py:14
  146.1 5.6 %collective-permute-start.19 = (f32[1,32,128]{2,1,0:T(8,128)S(1)}, f32[1,32,128]{2,1,0:T(8,128)S(1)}, u32[]{:S(2)}, u32[]{:S(2)}) collective-permute-start(f32[1,32,128]{2,1,0:T(8,128)S(1)} %get-tuple-element.335), channel_id=1, source_target_pairs={{16,0},{17,1},{18,2},{19,3},{20,4},{21,5},{22,6},{23,7},{24,8},{25... | collective-permute-start | bytes 49160 | tf_op jit(solution)/shard_map/ppermute | solution.py:17
  151.7 11.2 %collective-permute-start.20 = (f32[10,1,128]{2,1,0:T(1,128)S(1)}, f32[10,1,128]{2,1,0:T(1,128)S(1)}, u32[]{:S(2)}, u32[]{:S(2)}) collective-permute-start(f32[10,1,128]{2,1,0:T(1,128)S(1)} %get-tuple-element.332), channel_id=1, source_target_pairs={{0,4},{4,8},{8,12},{1,5},{5,9},{9,13},{2,6},{6,10},{10,14},{3,7},{... | collective-permute-start | bytes 15368 | tf_op jit(solution)/shard_map/ppermute | solution.py:14
  153.2 9.7 %collective-permute-start.21 = (f32[10,1,128]{2,1,0:T(1,128)S(1)}, f32[10,1,128]{2,1,0:T(1,128)S(1)}, u32[]{:S(2)}, u32[]{:S(2)}) collective-permute-start(f32[10,1,128]{2,1,0:T(1,128)S(1)} %get-tuple-element.333), channel_id=1, source_target_pairs={{4,0},{8,4},{12,8},{5,1},{9,5},{13,9},{6,2},{10,6},{14,10},{7,3},{... | collective-permute-start | bytes 15368 | tf_op jit(solution)/shard_map/ppermute | solution.py:17
  163.1 7.2 %collective-permute-start.22 = (f32[10,34,1]{2,1,0:T(8,128)S(1)}, f32[10,34,1]{2,1,0:T(8,128)S(1)}, u32[]{:S(2)}, u32[]{:S(2)}) collective-permute-start(f32[10,34,1]{2,1,0:T(8,128)S(1)} %get-tuple-element.330), channel_id=1, source_target_pairs={{0,1},{1,2},{2,3},{4,5},{5,6},{6,7},{8,9},{9,10},{10,11},{12,13},{... | collective-permute-start | bytes 4088 | tf_op jit(solution)/shard_map/ppermute | solution.py:14
  165.6 9.5 %collective-permute-start.23 = (f32[10,34,1]{2,1,0:T(8,128)S(1)}, f32[10,34,1]{2,1,0:T(8,128)S(1)}, u32[]{:S(2)}, u32[]{:S(2)}) collective-permute-start(f32[10,34,1]{2,1,0:T(8,128)S(1)} %get-tuple-element.331), channel_id=1, source_target_pairs={{1,0},{2,1},{3,2},{5,4},{6,5},{7,6},{9,8},{10,9},{11,10},{13,12},{... | collective-permute-start | bytes 4088 | tf_op jit(solution)/shard_map/ppermute | solution.py:17
  180.0 41.1 %copy-start.8 = (f32[9]{0:T(128)S(1)}, f32[9]{0:T(128)}, u32[]{:S(2)}) copy-start(f32[9]{0:T(128)} %constant.686.clone.1) | copy-start | bytes 112
  180.0 41.8 %copy-start.7 = (f32[9]{0:T(128)S(1)}, f32[9]{0:T(128)}, u32[]{:S(2)}) copy-start(f32[9]{0:T(128)} %constant.661.clone.1) | copy-start | bytes 112
  180.0 41.8 %copy-start.9 = (f32[9,1]{0,1:T(1,128)S(1)}, f32[9,1]{0,1:T(1,128)}, u32[]{:S(2)}) copy-start(f32[9,1]{0,1:T(1,128)} %constant.803) | copy-start | bytes 112
  (4 other events, 62.1 us)
where the time goes:
time: 262 us; the launch traced here: 260 us
  waiting for transfers between devices  61.3 us (23%)
  starting transfers between devices  48.7 us (19%)
  other arithmetic  43.5 us (17%)
  local copies, waits for them, and re-layouts  42.3 us (16%)
  blocking collectives  38.1 us (15%)
  between operations  15.9 us (6%)
  matrix products  10.1 us (4%)
    ppermute x12, waiting for transfers between devices, extended(): lax.ppermute(lax.slice_in_dim(block, 0, width, axis=dim), axis, backward)  39.2 us
    psum x1, blocking collectives, body(): gram = lax.psum(partial_gram, ('gx', 'gy', 'gz'))  38.1 us
    ppermute x12, starting transfers between devices, extended(): lax.ppermute(lax.slice_in_dim(block, block.shape[dim] - width, None, axis...  26.8 us
    gather x1, local copies, waits for them, and re-layouts, body(): incoming = jnp.take_along_axis(arrived, slot, axis=1)  25.6 us
    ppermute x12, waiting for transfers between devices, extended(): lax.ppermute(lax.slice_in_dim(block, block.shape[dim] - width, None, axis...  18.2 us
    ppermute x12, starting transfers between devices, extended(): lax.ppermute(lax.slice_in_dim(block, 0, width, axis=dim), axis, backward)  15.5 us
    add x2, other arithmetic, combine(): summed = summed + weights[position] * basis[position]  12.6 us
    mul x5, other arithmetic, operate(): result = capacity * values  7.02 us
  transfers between devices with their start and end apart: 25, of which 18 were waited for; matrix products, arithmetic and copies ran while one was open for 5% of the time, Pallas kernels for 0%

commit v1 on v0

--- a/solution.py
+++ b/solution.py
@@ -179,7 +179,7 @@
     basis = dir_terms + res_terms
     stacked = jnp.stack([term.reshape(-1) for term in basis])
     partial_gram = jnp.dot(stacked, stacked.T, precision=lax.Precision.HIGHEST)
-    gram = lax.psum(partial_gram, ("gx", "gy", "gz"))
+    gram = jnp.sum(lax.all_gather(partial_gram, ("gx", "gy", "gz")), axis=0)
     moved, residue, direct = coefficients(gram, center, half_width, STEPS)
     return (solution_in + combine(moved, basis), combine(residue, basis), combine(direct, basis))
 

time: 262 us -> 289 us (1.10)
  blocking collectives: 38.1 us -> 65.9 us
    all_gather x0 -> x1, blocking collectives: none -> 65.9 us  [body(): gram = jnp.sum(lax.all_gather(partial_gram, ('gx', 'gy', 'gz')), axis=0)]
    psum x1 -> x0, blocking collectives: 38.1 us -> none  [body(): gram = lax.psum(partial_gram, ('gx', 'gy', 'gz'))]
  transfers between devices with their start and end apart: 25 -> 25, of which waited for: 18 -> 18; matrix products, arithmetic and copies ran while one was open for 5% -> 4% of each run, Pallas kernels for 0% -> 0%
where the time goes in v1:
time: 289 us; the launch traced here: 288 us
  blocking collectives  65.9 us (23%)
  waiting for transfers between devices  61.3 us (21%)
  starting transfers between devices  48.7 us (17%)
  other arithmetic  43.6 us (15%)
  local copies, waits for them, and re-layouts  42.3 us (15%)
  between operations  16 us (6%)
  matrix products  10.1 us (3%)
    all_gather x1, blocking collectives, body(): gram = jnp.sum(lax.all_gather(partial_gram, ('gx', 'gy', 'gz')), axis=0)  65.9 us
    ppermute x12, waiting for transfers between devices, extended(): lax.ppermute(lax.slice_in_dim(block, 0, width, axis=dim), axis, backward)  39.2 us
    ppermute x12, starting transfers between devices, extended(): lax.ppermute(lax.slice_in_dim(block, block.shape[dim] - width, None, axis...  26.8 us
    gather x1, local copies, waits for them, and re-layouts, body(): incoming = jnp.take_along_axis(arrived, slot, axis=1)  25.6 us
    ppermute x12, waiting for transfers between devices, extended(): lax.ppermute(lax.slice_in_dim(block, block.shape[dim] - width, None, axis...  18.2 us
    ppermute x12, starting transfers between devices, extended(): lax.ppermute(lax.slice_in_dim(block, 0, width, axis=dim), axis, backward)  15.5 us
    add x2, other arithmetic, combine(): summed = summed + weights[position] * basis[position]  12.6 us
    mul x5, other arithmetic, operate(): result = capacity * values  7.02 us
  transfers between devices with their start and end apart: 25, of which 18 were waited for; matrix products, arithmetic and copies ran while one was open for 4% of the time, Pallas kernels for 0%

profile of v1, /device:TPU:0, one launch (start us, length us, event | category | flops | bytes accessed | tf_op | source)
XLA Modules:
  0.0 287.8 jit_solution(6593477849912700853)
XLA Ops:
  2.2 6.3 %all-to-all-start = ((f32[4,1,1024]{2,1,0:T(1,128)}), f32[4,1,1024]{2,1,0:T(1,128)S(1)}, u32[]{:S(2)}, u32[]{:S(2)}) async-start(f32[4,1,1024]{2,1,0:T(1,128)} %reshape.749), calls=%async_computation | async-start | bytes 32768 | tf_op jit(solution)/shard_map/all_to_all | solution.py:140
  10.2 3.9 %all-to-all-done = f32[4,1,1024]{2,1,0:T(1,128)S(1)} async-done(((f32[4,1,1024]{2,1,0:T(1,128)}), f32[4,1,1024]{2,1,0:T(1,128)S(1)}, u32[]{:S(2)}, u32[]{:S(2)}) %all-to-all-start) | async-done | bytes 16416 | tf_op jit(solution)/shard_map/all_to_all | solution.py:140
  15.6 25.6 %gather_fusion = f32[4096]{0:T(1024)S(1)} fusion(f32[32,128]{1,0:T(8,128)S(1)} %reshape.660, s32[4096]{0:T(1024)S(1)} %fusion.80), kind=kCustom, calls=%fused_computation | custom fusion | bytes 65536 | tf_op jit(solution)/shard_map/jit(take_along_axis)/gather | solution.py:153
  41.3 3.4 %collective-permute-start = (f32[3,1,32,128]{3,2,1,0:T(8,128)S(1)}, f32[3,1,32,128]{3,2,1,0:T(8,128)S(1)}, u32[]{:S(2)}, u32[]{:S(2)}) collective-permute-start(f32[3,1,32,128]{3,2,1,0:T(8,128)S(1)} %get-tuple-element.320), channel_id=1, source_target_pairs={{0,16},{1,17},{2,18},{3,19},{4,20},{5,21},{6,22},{7,23},{8,24},{9,... | collective-permute-start | bytes 147464 | tf_op jit(solution)/shard_map/ppermute | solution.py:14
  46.7 4.0 %collective-permute-done.1 = f32[3,1,32,128]{3,2,1,0:T(8,128)S(1)} collective-permute-done((f32[3,1,32,128]{3,2,1,0:T(8,128)S(1)}, f32[3,1,32,128]{3,2,1,0:T(8,128)S(1)}, u32[]{:S(2)}, u32[]{:S(2)}) %collective-permute-start.1) | collective-permute-done | bytes 49184 | tf_op jit(solution)/shard_map/ppermute | solution.py:17
  54.0 2.8 collective-permute-done.3
  57.4 2.6 collective-permute-start.4
  67.0 5.8 %bitcast_multiply_fusion.6 = (f32[10,34,130]{2,1,0:T(8,128)S(1)}, f32[1,10,34,130]{3,2,1,0:T(8,128)S(1)}, pred[1,10,34,130]{3,2,1,0:T(8,128)(4,1)S(1)}, pred[1,1...) fusion(f32[3,10,34,130]{3,2,1,0:T(8,128)S(1)} %pad_maximum_fusi, ...), kind=kLoop, calls=%fused_computation.86 | loop fusion | flops 1060800 | bytes 1060832 | tf_op jit(solution)/shard_map/mul | solution.py:40
  72.8 5.4 %add_add_fusion = f32[1,10,34,130]{3,2,1,0:T(8,128)S(1)} fusion(pred[1,10,34,130]{3,2,1,0:T(8,128)(4,1)S(1)} %get-tuple-element.283, pred[1,10,34,130]{3,2,1,0:T(8,128)(4,1)S(1)} %get-tuple-element.282, pred[1,10,34,130]{3,2,1,0:T(8,128)(4,1)S(1)} %get-tuple-element.281, pred[1,10,34,130]{3,2,1,0:T(8,128)(4,1)S(1)} %get-tuple-element.280, ...), kind=kLoop, calls=%fused_computation.87 | loop fusion | flops 663000 | bytes 530432 | tf_op jit(solution)/shard_map/add | solution.py:65
  82.8 4.2 %collective-permute-done.7 = f32[2,1,32,128]{3,2,1,0:T(8,128)S(1)} collective-permute-done((f32[2,1,32,128]{3,2,1,0:T(8,128)S(1)}, f32[2,1,32,128]{3,2,1,0:T(8,128)S(1)}, u32[]{:S(2)}, u32[]{:S(2)}) %collective-permute-start.7) | collective-permute-done | bytes 32800 | tf_op jit(solution)/shard_map/ppermute | solution.py:17
  87.1 2.4 collective-permute-start.8
  90.8 3.3 %collective-permute-done.9 = f32[2,10,1,128]{3,2,1,0:T(1,128)S(1)} collective-permute-done((f32[2,10,1,128]{3,2,1,0:T(1,128)S(1)}, f32[2,10,1,128]{3,2,1,0:T(1,128)S(1)}, u32[]{:S(2)}, u32[]{:S(2)}) %collective-permute-start.9) | collective-permute-done | bytes 10272 | tf_op jit(solution)/shard_map/ppermute | solution.py:17
  94.3 4.3 %collective-permute-start.10 = (f32[2,10,34,1]{3,2,1,0:T(8,128)S(1)}, f32[2,10,34,1]{3,2,1,0:T(8,128)S(1)}, u32[]{:S(2)}, u32[]{:S(2)}) collective-permute-start(f32[2,10,34,1]{3,2,1,0:T(8,128)S(1)} %get-tuple-element.318), channel_id=1, source_target_pairs={{0,1},{1,2},{2,3},{4,5},{5,6},{6,7},{8,9},{9,10},{10,11},{12,13},{... | collective-permute-start | bytes 8168 | tf_op jit(solution)/shard_map/ppermute | solution.py:14
  99.9 7.0 %collective-permute-done.10 = f32[2,10,34,1]{3,2,1,0:T(8,128)S(1)} collective-permute-done((f32[2,10,34,1]{3,2,1,0:T(8,128)S(1)}, f32[2,10,34,1]{3,2,1,0:T(8,128)S(1)}, u32[]{:S(2)}, u32[]{:S(2)}) %collective-permute-start.10) | collective-permute-done | bytes 2752 | tf_op jit(solution)/shard_map/ppermute | solution.py:14
  106.9 4.7 %collective-permute-done.11 = f32[2,10,34,1]{3,2,1,0:T(8,128)S(1)} collective-permute-done((f32[2,10,34,1]{3,2,1,0:T(8,128)S(1)}, f32[2,10,34,1]{3,2,1,0:T(8,128)S(1)}, u32[]{:S(2)}, u32[]{:S(2)}) %collective-permute-start.11) | collective-permute-done | bytes 2752 | tf_op jit(solution)/shard_map/ppermute | solution.py:17
  116.7 4.2 %collective-permute-done.13 = f32[2,1,32,128]{3,2,1,0:T(8,128)S(1)} collective-permute-done((f32[2,1,32,128]{3,2,1,0:T(8,128)S(1)}, f32[2,1,32,128]{3,2,1,0:T(8,128)S(1)}, u32[]{:S(2)}, u32[]{:S(2)}) %collective-permute-start.13) | collective-permute-done | bytes 32800 | tf_op jit(solution)/shard_map/ppermute | solution.py:17
  120.9 1.8 collective-permute-start.14
  124.0 1.9 collective-permute-done.15
  126.2 2.4 collective-permute-start.16
  129.9 7.0 %collective-permute-done.16 = f32[2,10,34,1]{3,2,1,0:T(8,128)S(1)} collective-permute-done((f32[2,10,34,1]{3,2,1,0:T(8,128)S(1)}, f32[2,10,34,1]{3,2,1,0:T(8,128)S(1)}, u32[]{:S(2)}, u32[]{:S(2)}) %collective-permute-start.16) | collective-permute-done | bytes 2752 | tf_op jit(solution)/shard_map/ppermute | solution.py:14
  136.9 4.7 %collective-permute-done.17 = f32[2,10,34,1]{3,2,1,0:T(8,128)S(1)} collective-permute-done((f32[2,10,34,1]{3,2,1,0:T(8,128)S(1)}, f32[2,10,34,1]{3,2,1,0:T(8,128)S(1)}, u32[]{:S(2)}, u32[]{:S(2)}) %collective-permute-start.17) | collective-permute-done | bytes 2752 | tf_op jit(solution)/shard_map/ppermute | solution.py:17
  147.5 4.2 %collective-permute-done.19 = f32[1,32,128]{2,1,0:T(8,128)S(1)} collective-permute-done((f32[1,32,128]{2,1,0:T(8,128)S(1)}, f32[1,32,128]{2,1,0:T(8,128)S(1)}, u32[]{:S(2)}, u32[]{:S(2)}) %collective-permute-start.19) | collective-permute-done | bytes 16416 | tf_op jit(solution)/shard_map/ppermute | solution.py:17
  156.1 1.9 dynamic-slice.147
  163.1 2.5 collective-permute-start.22
  167.0 3.3 %collective-permute-done.22 = f32[10,34,1]{2,1,0:T(8,128)S(1)} collective-permute-done((f32[10,34,1]{2,1,0:T(8,128)S(1)}, f32[10,34,1]{2,1,0:T(8,128)S(1)}, u32[]{:S(2)}, u32[]{:S(2)}) %collective-permute-start.22) | collective-permute-done | bytes 1392 | tf_op jit(solution)/shard_map/ppermute | solution.py:14
  170.3 4.7 %collective-permute-done.23 = f32[10,34,1]{2,1,0:T(8,128)S(1)} collective-permute-done((f32[10,34,1]{2,1,0:T(8,128)S(1)}, f32[10,34,1]{2,1,0:T(8,128)S(1)}, u32[]{:S(2)}, u32[]{:S(2)}) %collective-permute-start.23) | collective-permute-done | bytes 1392 | tf_op jit(solution)/shard_map/ppermute | solution.py:17
  178.1 1.9 stack.43
  180.0 2.9 %convolution_bitcast_fusion = f32[1,9,9]{2,1,0:T(8,128)S(1)} fusion(f32[9,32768]{1,0:T(8,128)S(1)} %stack.43), kind=kOutput, calls=%fused_computation.6 | convolution fusion | flops 31850496 | bytes 1179972 | tf_op jit(solution)/shard_map/dot_general | solution.py:181
  183.0 65.9 %all-gather.1 = f32[32,9,9]{2,1,0:T(8,128)S(1)} all-gather(f32[1,9,9]{2,1,0:T(8,128)S(1)} %convolution_bitcast_fusion), channel_id=2, replica_groups=mesh['gx'=2,'gy'=4,'gz'=4] {'gx','gy','gz'}, dimensions={0}, use_global_device_ids=true | all-gather | bytes 10692 | tf_op jit(solution)/shard_map/all_gather | solution.py:182
  268.8 6.2 %multiply_add_fusion = f32[8,32,128]{2,1,0:T(8,128)} fusion(f32[8,32,128]{2,1,0:T(8,128)S(1)} %fusion.54, f32[8,32,128]{2,1,0:T(8,128)S(1)} %fusion.66, f32[8,32,128]{2,1,0:T(8,128)S(1)} %get-tuple-element.383, f32[8,32,128]{2,1,0:T(8,128)S(1)} %fusion.78, f32[8,32,128]{2,1,0:T(8,128)S(1)} %fusion.58, f32[8,32,128]{2,1,0:T(8,128)S(1)} %fusion.62, ...), kind=kLoop, calls=%fused_computation.188 | loop fusion | flops 557056 | bytes 1310756 | tf_op jit(solution)/shard_map/add | solution.py:126
  275.0 6.4 %multiply_add_fusion.1 = f32[8,32,128]{2,1,0:T(8,128)} fusion(f32[8,32,128]{2,1,0:T(8,128)S(1)} %fusion.54, f32[8,32,128]{2,1,0:T(8,128)S(1)} %fusion.66, f32[8,32,128]{2,1,0:T(8,128)S(1)} %get-tuple-element.383, f32[8,32,128]{2,1,0:T(8,128)S(1)} %fusion.78, f32[8,32,128]{2,1,0:T(8,128)S(1)} %fusion.58, f32[8,32,128]{2,1,0:T(8,128)S(1)} %fusion.62, ...), kind=kLoop, calls=%fused_computation.189 | loop fusion | flops 557056 | bytes 1310756 | tf_op jit(solution)/shard_map/add | solution.py:126
  281.4 6.4 %add_add_fusion.2 = f32[8,32,128]{2,1,0:T(8,128)} fusion(f32[8,32,128]{2,1,0:T(8,128)S(1)} %copy-done.3, f32[8,32,128]{2,1,0:T(8,128)S(1)} %fusion.54, f32[8,32,128]{2,1,0:T(8,128)S(1)} %fusion.66, f32[8,32,128]{2,1,0:T(8,128)S(1)} %get-tuple-element.383, f32[8,32,128]{2,1,0:T(8,128)S(1)} %fusion.78, f32[8,32,128]{2,1,0:T(8,128)S(1)} %fusion.58, ...), kind=kLoop, calls=%fused_computation.190 | loop fusion | flops 589824 | bytes 1441828 | tf_op jit(solution)/shard_map/add | solution.py:184
  (162 shorter events, 57.8 us)
Async XLA Ops:
  2.2 11.9 %all-to-all-start = ((f32[4,1,1024]{2,1,0:T(1,128)}), f32[4,1,1024]{2,1,0:T(1,128)S(1)}, u32[]{:S(2)}, u32[]{:S(2)}) async-start(f32[4,1,1024]{2,1,0:T(1,128)} %reshape.749), calls=%async_computation | async-start | bytes 32768 | tf_op jit(solution)/shard_map/all_to_all | solution.py:140
  15.5 25.7 %copy-start = (f32[8,32,128]{2,1,0:T(8,128)S(1)}, f32[8,32,128]{2,1,0:T(8,128)}, u32[]{:S(2)}) copy-start(f32[8,32,128]{2,1,0:T(8,128)} %param.53) | copy-start | bytes 393220
  15.6 25.7 %copy-start.1 = (f32[8,32,128]{2,1,0:T(8,128)S(1)}, f32[8,32,128]{2,1,0:T(8,128)}, u32[]{:S(2)}) copy-start(f32[8,32,128]{2,1,0:T(8,128)} %param.54) | copy-start | bytes 393220
  15.6 30.4 %copy-start.5 = (f32[8]{0:T(128)S(1)}, f32[8]{0:T(128)}, u32[]{:S(2)}) copy-start(f32[8]{0:T(128)} %param.57) | copy-start | bytes 100
  15.6 37.7 %copy-start.6 = (f32[8]{0:T(128)S(1)}, f32[8]{0:T(128)}, u32[]{:S(2)}) copy-start(f32[8]{0:T(128)} %param.56) | copy-start | bytes 100
  41.3 5.4 %collective-permute-start = (f32[3,1,32,128]{3,2,1,0:T(8,128)S(1)}, f32[3,1,32,128]{3,2,1,0:T(8,128)S(1)}, u32[]{:S(2)}, u32[]{:S(2)}) collective-permute-start(f32[3,1,32,128]{3,2,1,0:T(8,128)S(1)} %get-tuple-element.320), channel_id=1, source_target_pairs={{0,16},{1,17},{2,18},{3,19},{4,20},{5,21},{6,22},{7,23},{8,24},{9,... | collective-permute-start | bytes 147464 | tf_op jit(solution)/shard_map/ppermute | solution.py:14
  44.7 6.0 %collective-permute-start.1 = (f32[3,1,32,128]{3,2,1,0:T(8,128)S(1)}, f32[3,1,32,128]{3,2,1,0:T(8,128)S(1)}, u32[]{:S(2)}, u32[]{:S(2)}) collective-permute-start(f32[3,1,32,128]{3,2,1,0:T(8,128)S(1)} %get-tuple-element.321), channel_id=1, source_target_pairs={{16,0},{17,1},{18,2},{19,3},{20,4},{21,5},{22,6},{23,7},{24,8},{25... | collective-permute-start | bytes 147464 | tf_op jit(solution)/shard_map/ppermute | solution.py:17
  50.7 3.3 %collective-permute-start.2 = (f32[3,10,1,128]{3,2,1,0:T(1,128)S(1)}, f32[3,10,1,128]{3,2,1,0:T(1,128)S(1)}, u32[]{:S(2)}, u32[]{:S(2)}) collective-permute-start(f32[3,10,1,128]{3,2,1,0:T(1,128)S(1)} %get-tuple-element.306), channel_id=1, source_target_pairs={{0,4},{4,8},{8,12},{1,5},{5,9},{9,13},{2,6},{6,10},{10,14},{3,7},{... | collective-permute-start | bytes 46088 | tf_op jit(solution)/shard_map/ppermute | solution.py:14
  52.0 4.8 %collective-permute-start.3 = (f32[3,10,1,128]{3,2,1,0:T(1,128)S(1)}, f32[3,10,1,128]{3,2,1,0:T(1,128)S(1)}, u32[]{:S(2)}, u32[]{:S(2)}) collective-permute-start(f32[3,10,1,128]{3,2,1,0:T(1,128)S(1)} %get-tuple-element.307), channel_id=1, source_target_pairs={{4,0},{8,4},{12,8},{5,1},{9,5},{13,9},{6,2},{10,6},{14,10},{7,3},{... | collective-permute-start | bytes 46088 | tf_op jit(solution)/shard_map/ppermute | solution.py:17
  57.4 7.8 %collective-permute-start.4 = (f32[3,10,34,1]{2,3,1,0:T(1,128)S(1)}, f32[3,10,34,1]{2,3,1,0:T(1,128)S(1)}, u32[]{:S(2)}, u32[]{:S(2)}) collective-permute-start(f32[3,10,34,1]{2,3,1,0:T(1,128)S(1)} %copy.31), channel_id=1, source_target_pairs={{0,1},{1,2},{2,3},{4,5},{5,6},{6,7},{8,9},{9,10},{10,11},{12,13},{... | collective-permute-start | bytes 12248 | tf_op jit(solution)/shard_map/ppermute | solution.py:14
  60.3 5.6 %collective-permute-start.5 = (f32[3,10,34,1]{2,3,1,0:T(1,128)S(1)}, f32[3,10,34,1]{2,3,1,0:T(1,128)S(1)}, u32[]{:S(2)}, u32[]{:S(2)}) collective-permute-start(f32[3,10,34,1]{2,3,1,0:T(1,128)S(1)} %copy.32), channel_id=1, source_target_pairs={{1,0},{2,1},{3,2},{5,4},{6,5},{7,6},{9,8},{10,9},{11,10},{13,12},{... | collective-permute-start | bytes 12248 | tf_op jit(solution)/shard_map/ppermute | solution.py:17
  79.7 3.2 %collective-permute-start.6 = (f32[2,1,32,128]{3,2,1,0:T(8,128)S(1)}, f32[2,1,32,128]{3,2,1,0:T(8,128)S(1)}, u32[]{:S(2)}, u32[]{:S(2)}) collective-permute-start(f32[2,1,32,128]{3,2,1,0:T(8,128)S(1)} %get-tuple-element.328), channel_id=1, source_target_pairs={{0,16},{1,17},{2,18},{3,19},{4,20},{5,21},{6,22},{7,23},{8,24},{9,... | collective-permute-start | bytes 98312 | tf_op jit(solution)/shard_map/ppermute | solution.py:14
  81.3 5.8 %collective-permute-start.7 = (f32[2,1,32,128]{3,2,1,0:T(8,128)S(1)}, f32[2,1,32,128]{3,2,1,0:T(8,128)S(1)}, u32[]{:S(2)}, u32[]{:S(2)}) collective-permute-start(f32[2,1,32,128]{3,2,1,0:T(8,128)S(1)} %get-tuple-element.329), channel_id=1, source_target_pairs={{16,0},{17,1},{18,2},{19,3},{20,4},{21,5},{22,6},{23,7},{24,8},{25... | collective-permute-start | bytes 98312 | tf_op jit(solution)/shard_map/ppermute | solution.py:17
  87.1 3.7 %collective-permute-start.8 = (f32[2,10,1,128]{3,2,1,0:T(1,128)S(1)}, f32[2,10,1,128]{3,2,1,0:T(1,128)S(1)}, u32[]{:S(2)}, u32[]{:S(2)}) collective-permute-start(f32[2,10,1,128]{3,2,1,0:T(1,128)S(1)} %get-tuple-element.324), channel_id=1, source_target_pairs={{0,4},{4,8},{8,12},{1,5},{5,9},{9,13},{2,6},{6,10},{10,14},{3,7},{... | collective-permute-start | bytes 30728 | tf_op jit(solution)/shard_map/ppermute | solution.py:14
  89.5 4.6 %collective-permute-start.9 = (f32[2,10,1,128]{3,2,1,0:T(1,128)S(1)}, f32[2,10,1,128]{3,2,1,0:T(1,128)S(1)}, u32[]{:S(2)}, u32[]{:S(2)}) collective-permute-start(f32[2,10,1,128]{3,2,1,0:T(1,128)S(1)} %get-tuple-element.325), channel_id=1, source_target_pairs={{4,0},{8,4},{12,8},{5,1},{9,5},{13,9},{6,2},{10,6},{14,10},{7,3},{... | collective-permute-start | bytes 30728 | tf_op jit(solution)/shard_map/ppermute | solution.py:17
  94.3 12.6 %collective-permute-start.10 = (f32[2,10,34,1]{3,2,1,0:T(8,128)S(1)}, f32[2,10,34,1]{3,2,1,0:T(8,128)S(1)}, u32[]{:S(2)}, u32[]{:S(2)}) collective-permute-start(f32[2,10,34,1]{3,2,1,0:T(8,128)S(1)} %get-tuple-element.318), channel_id=1, source_target_pairs={{0,1},{1,2},{2,3},{4,5},{5,6},{6,7},{8,9},{9,10},{10,11},{12,13},{... | collective-permute-start | bytes 8168 | tf_op jit(solution)/shard_map/ppermute | solution.py:14
  98.6 13.0 %collective-permute-start.11 = (f32[2,10,34,1]{3,2,1,0:T(8,128)S(1)}, f32[2,10,34,1]{3,2,1,0:T(8,128)S(1)}, u32[]{:S(2)}, u32[]{:S(2)}) collective-permute-start(f32[2,10,34,1]{3,2,1,0:T(8,128)S(1)} %get-tuple-element.319), channel_id=1, source_target_pairs={{1,0},{2,1},{3,2},{5,4},{6,5},{7,6},{9,8},{10,9},{11,10},{13,12},{... | collective-permute-start | bytes 8168 | tf_op jit(solution)/shard_map/ppermute | solution.py:17
  113.4 3.3 %collective-permute-start.12 = (f32[2,1,32,128]{3,2,1,0:T(8,128)S(1)}, f32[2,1,32,128]{3,2,1,0:T(8,128)S(1)}, u32[]{:S(2)}, u32[]{:S(2)}) collective-permute-start(f32[2,1,32,128]{3,2,1,0:T(8,128)S(1)} %get-tuple-element.326), channel_id=1, source_target_pairs={{0,16},{1,17},{2,18},{3,19},{4,20},{5,21},{6,22},{7,23},{8,24},{9,... | collective-permute-start | bytes 98312 | tf_op jit(solution)/shard_map/ppermute | solution.py:14
  115.0 5.9 %collective-permute-start.13 = (f32[2,1,32,128]{3,2,1,0:T(8,128)S(1)}, f32[2,1,32,128]{3,2,1,0:T(8,128)S(1)}, u32[]{:S(2)}, u32[]{:S(2)}) collective-permute-start(f32[2,1,32,128]{3,2,1,0:T(8,128)S(1)} %get-tuple-element.327), channel_id=1, source_target_pairs={{16,0},{17,1},{18,2},{19,3},{20,4},{21,5},{22,6},{23,7},{24,8},{25... | collective-permute-start | bytes 98312 | tf_op jit(solution)/shard_map/ppermute | solution.py:17
  120.9 3.1 %collective-permute-start.14 = (f32[2,10,1,128]{3,2,1,0:T(1,128)S(1)}, f32[2,10,1,128]{3,2,1,0:T(1,128)S(1)}, u32[]{:S(2)}, u32[]{:S(2)}) collective-permute-start(f32[2,10,1,128]{3,2,1,0:T(1,128)S(1)} %get-tuple-element.322), channel_id=1, source_target_pairs={{0,4},{4,8},{8,12},{1,5},{5,9},{9,13},{2,6},{6,10},{10,14},{3,7},{... | collective-permute-start | bytes 30728 | tf_op jit(solution)/shard_map/ppermute | solution.py:14
  122.7 3.2 %collective-permute-start.15 = (f32[2,10,1,128]{3,2,1,0:T(1,128)S(1)}, f32[2,10,1,128]{3,2,1,0:T(1,128)S(1)}, u32[]{:S(2)}, u32[]{:S(2)}) collective-permute-start(f32[2,10,1,128]{3,2,1,0:T(1,128)S(1)} %get-tuple-element.323), channel_id=1, source_target_pairs={{4,0},{8,4},{12,8},{5,1},{9,5},{13,9},{6,2},{10,6},{14,10},{7,3},{... | collective-permute-start | bytes 30728 | tf_op jit(solution)/shard_map/ppermute | solution.py:17
  126.2 10.7 %collective-permute-start.16 = (f32[2,10,34,1]{3,2,1,0:T(8,128)S(1)}, f32[2,10,34,1]{3,2,1,0:T(8,128)S(1)}, u32[]{:S(2)}, u32[]{:S(2)}) collective-permute-start(f32[2,10,34,1]{3,2,1,0:T(8,128)S(1)} %get-tuple-element.312), channel_id=1, source_target_pairs={{0,1},{1,2},{2,3},{4,5},{5,6},{6,7},{8,9},{9,10},{10,11},{12,13},{... | collective-permute-start | bytes 8168 | tf_op jit(solution)/shard_map/ppermute | solution.py:14
  128.6 13.0 %collective-permute-start.17 = (f32[2,10,34,1]{3,2,1,0:T(8,128)S(1)}, f32[2,10,34,1]{3,2,1,0:T(8,128)S(1)}, u32[]{:S(2)}, u32[]{:S(2)}) collective-permute-start(f32[2,10,34,1]{3,2,1,0:T(8,128)S(1)} %get-tuple-element.313), channel_id=1, source_target_pairs={{1,0},{2,1},{3,2},{5,4},{6,5},{7,6},{9,8},{10,9},{11,10},{13,12},{... | collective-permute-start | bytes 8168 | tf_op jit(solution)/shard_map/ppermute | solution.py:17
  144.4 3.0 %collective-permute-start.18 = (f32[1,32,128]{2,1,0:T(8,128)S(1)}, f32[1,32,128]{2,1,0:T(8,128)S(1)}, u32[]{:S(2)}, u32[]{:S(2)}) collective-permute-start(f32[1,32,128]{2,1,0:T(8,128)S(1)} %get-tuple-element.334), channel_id=1, source_target_pairs={{0,16},{1,17},{2,18},{3,19},{4,20},{5,21},{6,22},{7,23},{8,24},{9,... | collective-permute-start | bytes 49160 | tf_op jit(solution)/shard_map/ppermute | solution.py:14
  146.1 5.6 %collective-permute-start.19 = (f32[1,32,128]{2,1,0:T(8,128)S(1)}, f32[1,32,128]{2,1,0:T(8,128)S(1)}, u32[]{:S(2)}, u32[]{:S(2)}) collective-permute-start(f32[1,32,128]{2,1,0:T(8,128)S(1)} %get-tuple-element.335), channel_id=1, source_target_pairs={{16,0},{17,1},{18,2},{19,3},{20,4},{21,5},{22,6},{23,7},{24,8},{25... | collective-permute-start | bytes 49160 | tf_op jit(solution)/shard_map/ppermute | solution.py:17
  151.7 11.2 %collective-permute-start.20 = (f32[10,1,128]{2,1,0:T(1,128)S(1)}, f32[10,1,128]{2,1,0:T(1,128)S(1)}, u32[]{:S(2)}, u32[]{:S(2)}) collective-permute-start(f32[10,1,128]{2,1,0:T(1,128)S(1)} %get-tuple-element.332), channel_id=1, source_target_pairs={{0,4},{4,8},{8,12},{1,5},{5,9},{9,13},{2,6},{6,10},{10,14},{3,7},{... | collective-permute-start | bytes 15368 | tf_op jit(solution)/shard_map/ppermute | solution.py:14
  153.2 9.7 %collective-permute-start.21 = (f32[10,1,128]{2,1,0:T(1,128)S(1)}, f32[10,1,128]{2,1,0:T(1,128)S(1)}, u32[]{:S(2)}, u32[]{:S(2)}) collective-permute-start(f32[10,1,128]{2,1,0:T(1,128)S(1)} %get-tuple-element.333), channel_id=1, source_target_pairs={{4,0},{8,4},{12,8},{5,1},{9,5},{13,9},{6,2},{10,6},{14,10},{7,3},{... | collective-permute-start | bytes 15368 | tf_op jit(solution)/shard_map/ppermute | solution.py:17
  163.1 7.2 %collective-permute-start.22 = (f32[10,34,1]{2,1,0:T(8,128)S(1)}, f32[10,34,1]{2,1,0:T(8,128)S(1)}, u32[]{:S(2)}, u32[]{:S(2)}) collective-permute-start(f32[10,34,1]{2,1,0:T(8,128)S(1)} %get-tuple-element.330), channel_id=1, source_target_pairs={{0,1},{1,2},{2,3},{4,5},{5,6},{6,7},{8,9},{9,10},{10,11},{12,13},{... | collective-permute-start | bytes 4088 | tf_op jit(solution)/shard_map/ppermute | solution.py:14
  165.6 9.5 %collective-permute-start.23 = (f32[10,34,1]{2,1,0:T(8,128)S(1)}, f32[10,34,1]{2,1,0:T(8,128)S(1)}, u32[]{:S(2)}, u32[]{:S(2)}) collective-permute-start(f32[10,34,1]{2,1,0:T(8,128)S(1)} %get-tuple-element.331), channel_id=1, source_target_pairs={{1,0},{2,1},{3,2},{5,4},{6,5},{7,6},{9,8},{10,9},{11,10},{13,12},{... | collective-permute-start | bytes 4088 | tf_op jit(solution)/shard_map/ppermute | solution.py:17
  180.0 68.9 %copy-start.8 = (f32[9]{0:T(128)S(1)}, f32[9]{0:T(128)}, u32[]{:S(2)}) copy-start(f32[9]{0:T(128)} %constant.686.clone.1) | copy-start | bytes 112
  180.0 69.6 %copy-start.7 = (f32[9]{0:T(128)S(1)}, f32[9]{0:T(128)}, u32[]{:S(2)}) copy-start(f32[9]{0:T(128)} %constant.661.clone.1) | copy-start | bytes 112
  180.0 69.6 %copy-start.9 = (f32[9,1]{0,1:T(1,128)S(1)}, f32[9,1]{0,1:T(1,128)}, u32[]{:S(2)}) copy-start(f32[9,1]{0,1:T(1,128)} %constant.803) | copy-start | bytes 112
  (4 other events, 62.1 us)
